TPU v7x, 32 devices: a whole 2x2x4 slice. The times are simulated.
32 devices in a mesh: dp: 4 (over y, x), tp: 8 (over z, core).
Axes of the slice: x: 2, y: 2, z: 4, core: 2. Of those that a mesh axis runs over, the one named last changes fastest.
Arguments:
- hidden_in: bfloat16 [4, 32, 4096], P(None, 'dp'), may hold values from -6 to 6
- pre_gain: float32 [4096], replicated, may hold values from 0.25 to 1.75
- w_zx: bfloat16 [4096, 2, 8192], P(None, None, 'tp'), may hold values from -0.09375 to 0.09375
- zx_codes: bfloat16 [4096, 2, 8192], P(('dp', 'tp')), may hold values from -4 to 4
- zx_exponents: int32 [32, 2, 64], P('dp', None, 'tp'), may hold values from -9 to -6
- w_bc: bfloat16 [4096, 2048], P(None, 'tp'), may hold values from -0.09375 to 0.09375
- w_dt: bfloat16 [4096, 128], P(None, 'tp'), may hold values from -0.09375 to 0.09375
- conv_x: float32 [5, 8192], P(None, 'tp'), may hold values from -0.6 to 0.6
- conv_bc: float32 [5, 2048], P(None, 'tp'), may hold values from -0.6 to 0.6
- dt_bias: float32 [128], P('tp'), may hold values from -2 to 0.5
- decay_rate: float32 [128], P('tp'), may hold values from 0.05 to 2
- skip_gain: float32 [128], P('tp'), may hold values from 0.5 to 1.5
- conv_state_x: bfloat16 [32, 3, 8192], P('dp', None, 'tp'), may hold values from -6 to 6
- conv_state_bc: bfloat16 [32, 3, 2048], P('dp', None, 'tp'), may hold values from -6 to 6
- ssm_state: float32 [32, 128, 64, 256], P('dp', 'tp'), may hold values from -6 to 6
- norm_gain: float32 [8192], P('tp'), may hold values from 0.25 to 1.75
- w_out: bfloat16 [8192, 4096], P('tp'), may hold values from -0.0625 to 0.0625
- out_codes: bfloat16 [8192, 4096], P('tp', 'dp'), may hold values from -4 to 4
- out_exponents: int32 [64, 32], P('tp', 'dp'), may hold values from -7 to -4
Outputs:
- mixed: bfloat16 [4, 32, 4096], P(None, 'dp', 'tp')
- final_state: float32 [32, 128, 64, 256], P('dp', 'tp')
All inputs are finite; a program needn't handle non-finite values.
Results may differ from a plain program's by a relative error of at most 0.014.
Values may be sent and summed in bfloat16 or wider, within the bound.
A program may use at most 192 MiB of HBM per device.

v0:
```python
import jax
import jax.numpy as jnp
from jax import lax
from jax.sharding import PartitionSpec as P

D = 4096
H = 128
G = 4
BLK = 128
STEPS = 4
DI = 8192
EPS = 1e-05


def decode_pairs(codes, exponents, block):
    rows, pair, cols = codes.shape
    blocked = codes.astype(jnp.float32).reshape(rows // block, block, pair, cols // block, block)
    scales = jnp.exp2(exponents.astype(jnp.float32))
    return (blocked * scales[:, None, :, :, None]).reshape(rows, pair, cols)


def decode_matrix(codes, exponents, block):
    rows, cols = codes.shape
    blocked = codes.astype(jnp.float32).reshape(rows // block, block, cols // block, block)
    scales = jnp.exp2(exponents.astype(jnp.float32))
    return (blocked * scales[:, None, :, None]).reshape(rows, cols)


def conv_step(history, fresh, params):
    window = jnp.concatenate([history, fresh[:, None, :]], axis=1)
    mixed = jnp.sum(window * params[:4][None], axis=1) + params[4]
    return (jax.nn.silu(mixed), window[:, 1:])


def body(
    hidden_in,
    pre_gain,
    w_zx,
    zx_codes,
    zx_exponents,
    w_bc,
    w_dt,
    conv_x,
    conv_bc,
    dt_bias,
    decay_rate,
    skip_gain,
    conv_state_x,
    conv_state_bc,
    ssm_state,
    norm_gain,
    w_out,
    out_codes,
    out_exponents,
):
    slot = lax.axis_index("tp")
    tp_count = lax.axis_size("tp")
    traded = lax.all_to_all(zx_codes, "tp", split_axis=2, concat_axis=0, tiled=True)
    zx_delta = decode_pairs(traded, zx_exponents, BLK)
    local_cols = traded.shape[2]
    gathered = lax.all_gather(zx_delta.astype(jnp.bfloat16), "dp", axis=0, tiled=True)
    zx_weights = (
        (w_zx.astype(jnp.float32) + gathered.astype(jnp.float32))
        .astype(jnp.bfloat16)
        .reshape(D, 2 * local_cols)
    )
    out_piece = decode_matrix(out_codes, out_exponents, BLK).astype(jnp.bfloat16)
    out_full = lax.all_gather(out_piece, "dp", axis=1, tiled=True)
    new_out = (w_out.astype(jnp.float32) + out_full.astype(jnp.float32)).astype(jnp.bfloat16)
    heads_here = ssm_state.shape[1]
    states_n = ssm_state.shape[3]
    group = slot * heads_here // (H // G)
    group_mask = (jnp.arange(G) == group).astype(jnp.float32)
    history_x = conv_state_x.astype(jnp.float32)
    history_bc = conv_state_bc.astype(jnp.float32)
    state = ssm_state
    results = []
    carried = None
    for step in range(STEPS):
        x = hidden_in[step].astype(jnp.float32)
        if step > 0:
            x = x + carried.astype(jnp.float32)
        rows = x.shape[0]
        normed = (x * lax.rsqrt(jnp.mean(x * x, -1, keepdims=True) + EPS) * pre_gain).astype(
            jnp.bfloat16
        )
        zx = jnp.dot(normed, zx_weights, preferred_element_type=jnp.float32)
        zx = zx.reshape(rows, 2, local_cols)
        gate = zx[:, 0]
        inner = zx[:, 1]
        bc_raw = jnp.dot(normed, w_bc, preferred_element_type=jnp.float32)
        dt_raw = jnp.dot(normed, w_dt, preferred_element_type=jnp.float32)
        conv_inner, history_x = conv_step(history_x, inner, conv_x)
        conv_piece, history_bc = conv_step(history_bc, bc_raw, conv_bc)
        bc_all = lax.all_gather(conv_piece, "tp", axis=1, tiled=True)
        b_group = lax.dynamic_slice_in_dim(bc_all, group * states_n, states_n, 1)
        c_group = lax.dynamic_slice_in_dim(bc_all, G * states_n + group * states_n, states_n, 1)
        step_size = jax.nn.softplus(dt_raw + dt_bias)
        decay = jnp.exp(-step_size * decay_rate)
        inner_heads = conv_inner.reshape(rows, heads_here, -1)
        state = (
            decay[:, :, None, None] * state
            + (step_size[:, :, None] * inner_heads)[:, :, :, None] * b_group[:, None, None, :]
        )
        read = (
            jnp.einsum("rhpn,rn->rhp", state, c_group, precision=lax.Precision.HIGHEST)
            + skip_gain[:, None] * inner_heads
        )
        gated = read.reshape(rows, local_cols) * jax.nn.silu(gate)
        squares = jnp.sum(gated * gated, -1)
        totals = lax.psum(squares[:, None] * group_mask, "tp")
        mean_sq = jnp.sum(totals * group_mask, -1) / (DI // G)
        scaled = (gated * lax.rsqrt(mean_sq + EPS)[:, None] * norm_gain).astype(jnp.bfloat16)
        partial_value = jnp.dot(scaled, new_out, preferred_element_type=jnp.float32)
        whole = lax.psum(partial_value, "tp").astype(jnp.bfloat16)
        width = partial_value.shape[1] // tp_count
        results.append(lax.dynamic_slice_in_dim(whole, slot * width, width, 1))
        carried = whole
    return (jnp.stack(results), state)


def solution(mesh):
    return jax.shard_map(
        body,
        mesh=mesh,
        in_specs=(
            P(None, "dp", None),
            P(),
            P(None, None, "tp"),
            P(("dp", "tp"), None, None),
            P("dp", None, "tp"),
            P(None, "tp"),
            P(None, "tp"),
            P(None, "tp"),
            P(None, "tp"),
            P("tp"),
            P("tp"),
            P("tp"),
            P("dp", None, "tp"),
            P("dp", None, "tp"),
            P("dp", "tp", None, None),
            P("tp"),
            P("tp", None),
            P("tp", "dp"),
            P("tp", "dp"),
        ),
        out_specs=(P(None, "dp", "tp"), P("dp", "tp", None, None)),
        check_vma=False,
    )
```

profile of v0, /device:TPU:0, one launch (start us, length us, event | category | flops | bytes accessed | tf_op | source)
XLA Modules:
  0.0 712.7 jit_solution(7525767807919478908)
XLA Ops:
  12.6 15.0 %copy.29 = bf16[128,2,8192]{0,1,2:T(2,128)(2,1)} copy(bf16[128,2,8192]{2,1,0:T(2,128)(2,1)} %param.22) | data formatting | bytes 8388608 | tf_op args[3]
  38.1 10.8 %mul.610 = f32[1024,2,1024]{2,1,0:T(2,128)} reshape(f32[8,128,2,8,128]{4,3,2,1,0:T(8,128)} %mul.609) | data formatting | bytes 16777216 | tf_op jit(solution)/shard_map/mul | solution.py:19
  48.8 79.2 %all-to-all-done = bf16[128,2,8192]{0,1,2:T(2,128)(2,1)} async-done(((bf16[128,2,8192]{0,1,2:T(2,128)(2,1)}), bf16[128,2,8192]{0,1,2:T(2,128)(2,1)}, u32[]{:S(2)}, u32[]{:S(2)}) %all-to-all-start) | async-done | bytes 4194336 | tf_op jit(solution)/shard_map/all_to_all | solution.py:58
  136.5 17.1 %copy.30 = f32[8,128,2,1024]{3,2,1,0:T(2,128)} copy(f32[8,128,2,1024]{1,2,3,0:T(2,128)} %convert_bitcast_fusion) | data formatting | bytes 16777216 | tf_op jit(solution)/shard_map/convert_element_type | solution.py:17
  163.6 14.2 %all_gather.19 = f32[8,2048]{1,0:T(8,128)S(1)} all-gather(f32[8,256]{1,0:T(8,128)S(1)} %divide_multiply_fusion.7), channel_id=1, replica_groups=mesh['dp'=4,'tp'=8] {'tp'}, dimensions={1}, use_global_device_ids=true | all-gather | bytes 73728 | tf_op jit(solution)/shard_map/all_gather | solution.py:95
  188.2 131.0 %all-gather.3.cloned.1.call-done = bf16[4096,2,1024]{2,1,0:T(2,128)(2,1)} async-done(((bf16[1024,2,1024]{2,1,0:T(2,128)(2,1)}), bf16[4096,2,1024]{2,1,0:T(2,128)(2,1)}) %all-gather.3.cloned.1.call-update) | async-done | bytes 16777232 | tf_op jit(solution)/shard_map/all_gather | solution.py:61
  319.1 19.2 %add_convert_fusion = bf16[4096,2,1024]{2,1,0:T(2,128)(2,1)S(1)} fusion(bf16[4096,2,1024]{2,1,0:T(2,128)(2,1)} %all-gather.3.cloned.1.call-done, bf16[4096,2,1024]{2,1,0:T(2,128)(2,1)} %param.21), kind=kLoop, calls=%fused_computation | loop fusion | flops 33554432 | bytes 50331648 | tf_op jit(solution)/shard_map/convert_element_type | solution.py:64
  347.6 20.7 %copy.31 = bf16[2048,4096]{1,0:T(8,128)(2,1)} copy(bf16[2048,4096]{0,1:T(8,128)(2,1)} %bitcast.211) | data formatting | bytes 33554432 | tf_op jit(solution)/shard_map/dot_general | solution.py:87
  378.8 13.1 %fusion.1 = f32[8,1,16,64]{3,1,2,0:T(1,128)S(1)} fusion(f32[8,16,64,256]{3,2,1,0:T(8,128)} %param.33, f32[8,256]{1,0:T(8,128)S(1)} %get-tuple-element.23, f32[8,16,64]{2,1,0:T(8,128)S(1)} %broadcast_multiply_fusion.3, f32[8,16]{1,0:T(8,128)S(1)} %get-tuple-element.26, f32[8,256,1,1]{1,0,2,3:T(8,128)S(1)} %get-tuple-element.22), kind=kOutput, calls=%fused_computation.9 | convolution fusion | flops 31457280 | bytes 8471040 | tf_op jit(solution)/shard_map/rhpn,rn->rhp/dot_general | solution.py:106
  392.2 16.4 %psum.56 = f32[8,4]{0,1:T(4,128)S(1)} all-reduce(f32[8,4]{0,1:T(4,128)S(1)} %broadcast_multiply_fusion.7), channel_id=1, replica_groups=mesh['dp'=4,'tp'=8] {'tp'}, use_global_device_ids=true, to_apply=%region_4.5 | all-reduce | flops 32 | bytes 256 | tf_op jit(solution)/shard_map/psum | solution.py:111
  413.4 27.1 %all-reduce.4 = bf16[8,4096]{1,0:T(8,128)(2,1)S(1)} all-reduce(f32[8,4096]{1,0:T(8,128)S(1)} %fusion.84), channel_id=1, replica_groups=mesh['dp'=4,'tp'=8] {'tp'}, use_global_device_ids=true, to_apply=%region_6.7 | all-reduce | flops 32768 | bytes 196608 | tf_op jit(solution)/shard_map/psum | solution.py:115
  440.8 10.2 %fusion.35 = f32[8,2,1024]{2,0,1:T(8,128)S(1)} fusion(bf16[2,1024,4096]{2,1,0:T(8,128)(2,1)} %bitcast.207, bf16[8,4096]{1,0:T(8,128)(2,1)S(1)} %multiply_convert_fusion.2), kind=kOutput, calls=%fused_computation.72 | convolution fusion | flops 134217728 | bytes 16908288 | tf_op jit(solution)/shard_map/dot_general | solution.py:87
  451.7 14.0 %all_gather.21 = f32[8,2048]{1,0:T(8,128)S(1)} all-gather(f32[8,256]{1,0:T(8,128)S(1)} %divide_multiply_fusion.6), channel_id=1, replica_groups=mesh['dp'=4,'tp'=8] {'tp'}, dimensions={1}, use_global_device_ids=true | all-gather | bytes 73728 | tf_op jit(solution)/shard_map/all_gather | solution.py:95
  465.9 13.7 %fusion.10 = f32[8,1,16,64]{3,1,2,0:T(1,128)S(1)} fusion(f32[8,16,64,256]{3,2,1,0:T(8,128)} %param.33, f32[8,256]{1,0:T(8,128)S(1)} %get-tuple-element.19, f32[8,16,64]{2,1,0:T(8,128)S(1)} %broadcast_multiply_fusion.2, f32[8,16]{1,0:T(8,128)S(1)} %get-tuple-element.28, f32[8,256]{1,0:T(8,128)S(1)} %get-tuple-element.23, ...), kind=kOutput, calls=%fused_computation.19 | convolution fusion | flops 37748736 | bytes 8512512 | tf_op jit(solution)/shard_map/rhpn,rn->rhp/dot_general | solution.py:106
  479.9 13.9 %psum.58 = f32[8,4]{0,1:T(4,128)S(1)} all-reduce(f32[8,4]{0,1:T(4,128)S(1)} %broadcast_multiply_fusion.6), channel_id=1, replica_groups=mesh['dp'=4,'tp'=8] {'tp'}, use_global_device_ids=true, to_apply=%region_11.12 | all-reduce | flops 32 | bytes 256 | tf_op jit(solution)/shard_map/psum | solution.py:111
  498.6 27.7 %all-reduce.5 = bf16[8,4096]{1,0:T(8,128)(2,1)S(1)} all-reduce(f32[8,4096]{1,0:T(8,128)S(1)} %fusion.82), channel_id=1, replica_groups=mesh['dp'=4,'tp'=8] {'tp'}, use_global_device_ids=true, to_apply=%region_13.14 | all-reduce | flops 32768 | bytes 196608 | tf_op jit(solution)/shard_map/psum | solution.py:115
  526.5 10.2 %fusion.33 = f32[8,2,1024]{2,0,1:T(8,128)S(1)} fusion(bf16[2,1024,4096]{2,1,0:T(8,128)(2,1)} %bitcast.208, bf16[8,4096]{1,0:T(8,128)(2,1)S(1)} %multiply_convert_fusion.1), kind=kOutput, calls=%fused_computation.70 | convolution fusion | flops 134217728 | bytes 16908288 | tf_op jit(solution)/shard_map/dot_general | solution.py:87
  537.4 14.0 %all_gather.22 = f32[8,2048]{1,0:T(8,128)S(1)} all-gather(f32[8,256]{1,0:T(8,128)S(1)} %divide_multiply_fusion.5), channel_id=1, replica_groups=mesh['dp'=4,'tp'=8] {'tp'}, dimensions={1}, use_global_device_ids=true | all-gather | bytes 73728 | tf_op jit(solution)/shard_map/all_gather | solution.py:95
  551.6 14.5 %fusion.2 = f32[8,1,16,64]{3,1,2,0:T(1,128)S(1)} fusion(f32[8,256]{1,0:T(8,128)S(1)} %get-tuple-element.15, f32[8,16,64]{2,1,0:T(8,128)S(1)} %broadcast_multiply_fusion.1, f32[8,16]{1,0:T(8,128)S(1)} %get-tuple-element.30, f32[8,16,64,256]{3,2,1,0:T(8,128)} %param.33, f32[8,256]{1,0:T(8,128)S(1)} %get-tuple-element.19, ...), kind=kOutput, calls=%fused_computation.10 | convolution fusion | flops 44040192 | bytes 8553984 | tf_op jit(solution)/shard_map/rhpn,rn->rhp/dot_general | solution.py:106
  566.4 13.9 %psum.60 = f32[8,4]{0,1:T(4,128)S(1)} all-reduce(f32[8,4]{0,1:T(4,128)S(1)} %broadcast_multiply_fusion.5), channel_id=1, replica_groups=mesh['dp'=4,'tp'=8] {'tp'}, use_global_device_ids=true, to_apply=%region_18.19 | all-reduce | flops 32 | bytes 256 | tf_op jit(solution)/shard_map/psum | solution.py:111
  585.1 27.2 %all-reduce.6 = bf16[8,4096]{1,0:T(8,128)(2,1)S(1)} all-reduce(f32[8,4096]{1,0:T(8,128)S(1)} %fusion.80), channel_id=1, replica_groups=mesh['dp'=4,'tp'=8] {'tp'}, use_global_device_ids=true, to_apply=%region_20.21 | all-reduce | flops 32768 | bytes 196608 | tf_op jit(solution)/shard_map/psum | solution.py:115
  623.5 14.2 %all_gather.23 = f32[8,2048]{1,0:T(8,128)S(1)} all-gather(f32[8,256]{1,0:T(8,128)S(1)} %divide_multiply_fusion.4), channel_id=1, replica_groups=mesh['dp'=4,'tp'=8] {'tp'}, dimensions={1}, use_global_device_ids=true | all-gather | bytes 73728 | tf_op jit(solution)/shard_map/all_gather | solution.py:95
  659.1 13.9 %psum.62 = f32[8,4]{0,1:T(4,128)S(1)} all-reduce(f32[8,4]{0,1:T(4,128)S(1)} %broadcast_multiply_fusion.4), channel_id=1, replica_groups=mesh['dp'=4,'tp'=8] {'tp'}, use_global_device_ids=true, to_apply=%region_25.26 | all-reduce | flops 32 | bytes 256 | tf_op jit(solution)/shard_map/psum | solution.py:111
  677.8 27.2 %all-reduce.7 = bf16[8,4096]{1,0:T(8,128)(2,1)S(1)} all-reduce(f32[8,4096]{1,0:T(8,128)S(1)} %fusion.78), channel_id=1, replica_groups=mesh['dp'=4,'tp'=8] {'tp'}, use_global_device_ids=true, to_apply=%region_27.28 | all-reduce | flops 32768 | bytes 196608 | tf_op jit(solution)/shard_map/psum | solution.py:115
  (141 shorter events, 119.7 us)
Async XLA Ops:
  7.2 156.0 %copy-start = (bf16[4096,256]{1,0:T(8,128)(2,1)S(1)}, bf16[4096,256]{1,0:T(8,128)(2,1)}, u32[]{:S(2)}) copy-start(bf16[4096,256]{1,0:T(8,128)(2,1)} %param.24) | copy-start | bytes 6291460
  7.2 170.9 %all-gather.5.cloned.1.call-start = ((), (), s32[]{:S(2)}) async-start(), calls=%async_computation.2 | async-start | bytes 10485760 | tf_op jit(solution)/shard_map/all_gather | solution.py:68
  12.6 21.5 %copy-start.10 = (s32[8,2,8]{2,1,0:T(2,128)S(1)}, s32[8,2,8]{2,1,0:T(2,128)}, u32[]{:S(2)}) copy-start(s32[8,2,8]{2,1,0:T(2,128)} %param.23) | copy-start | bytes 1540
  27.6 100.5 %all-to-all-start = ((bf16[128,2,8192]{0,1,2:T(2,128)(2,1)}), bf16[128,2,8192]{0,1,2:T(2,128)(2,1)}, u32[]{:S(2)}, u32[]{:S(2)}) async-start(bf16[128,2,8192]{0,1,2:T(2,128)(2,1)} %copy.29), calls=%async_computation | async-start | bytes 8388608 | tf_op jit(solution)/shard_map/all_to_all | solution.py:58
  34.0 285.2 %all-gather.3.cloned.1.call-start = ((), (), s32[]{:S(2)}) async-start(), calls=%async_computation.1 | async-start | bytes 20971520 | tf_op jit(solution)/shard_map/all_gather | solution.py:61
  153.6 9.1 %copy-start.13 = (f32[5,256]{1,0:T(8,128)S(1)}, f32[5,256]{1,0:T(8,128)}, u32[]{:S(2)}) copy-start(f32[5,256]{1,0:T(8,128)} %param.27) | copy-start | bytes 15364
  153.6 9.2 %copy-start.8 = (bf16[8,3,256]{2,0,1:T(8,128)(2,1)S(1)}, bf16[8,3,256]{2,0,1:T(8,128)(2,1)}, u32[]{:S(2)}) copy-start(bf16[8,3,256]{2,0,1:T(8,128)(2,1)} %param.32) | copy-start | bytes 36868
  153.6 9.2 %copy-start.7 = (f32[5,1024]{1,0:T(8,128)S(1)}, f32[5,1024]{1,0:T(8,128)}, u32[]{:S(2)}) copy-start(f32[5,1024]{1,0:T(8,128)} %param.26) | copy-start | bytes 61444
  153.6 9.2 %copy-start.6 = (bf16[8,3,1024]{2,0,1:T(8,128)(2,1)S(1)}, bf16[8,3,1024]{2,0,1:T(8,128)(2,1)}, u32[]{:S(2)}) copy-start(bf16[8,3,1024]{2,0,1:T(8,128)(2,1)} %param.31) | copy-start | bytes 147460
  153.6 9.3 %copy-start.2 = (bf16[4,8,4096]{2,1,0:T(8,128)(2,1)S(1)}, bf16[4,8,4096]{2,1,0:T(8,128)(2,1)}, u32[]{:S(2)}) copy-start(bf16[4,8,4096]{2,1,0:T(8,128)(2,1)} %param.19) | copy-start | bytes 786436
  153.6 9.5 %copy-start.5 = (f32[4096]{0:T(1024)S(1)}, f32[4096]{0:T(1024)}, u32[]{:S(2)}) copy-start(f32[4096]{0:T(1024)} %param.20) | copy-start | bytes 49156
  153.7 24.1 %copy-start.3 = (bf16[4096,16]{0,1:T(8,128)(2,1)S(1)}, bf16[4096,16]{0,1:T(8,128)(2,1)}, u32[]{:S(2)}) copy-start(bf16[4096,16]{0,1:T(8,128)(2,1)} %param.25) | copy-start | bytes 393220
  153.7 24.1 %copy-start.11 = (f32[16]{0:T(128)S(1)}, f32[16]{0:T(128)}, u32[]{:S(2)}) copy-start(f32[16]{0:T(128)} %param.29) | copy-start | bytes 196
  153.7 24.1 %copy-start.12 = (f32[16]{0:T(128)S(1)}, f32[16]{0:T(128)}, u32[]{:S(2)}) copy-start(f32[16]{0:T(128)} %param.28) | copy-start | bytes 196
  378.5 13.4 %copy-start.9 = (f32[16]{0:T(128)S(1)}, f32[16]{0:T(128)}, u32[]{:S(2)}) copy-start(f32[16]{0:T(128)} %param.30) | copy-start | bytes 196
  378.5 30.2 %copy-start.4 = (f32[1024]{0:T(1024)S(1)}, f32[1024]{0:T(1024)}, u32[]{:S(2)}) copy-start(f32[1024]{0:T(1024)} %param.34) | copy-start | bytes 12292
  645.5 3.4 copy-start.1
Sparse Core Ops, SparseCore 0:
  12.7 90.1 all-gather.4
  162.9 156.2 all-gather.2
where the time goes:
time: 721 us; the launch traced here: 713 us
  blocking collectives  224 us (31%)
  waiting for transfers between devices  210 us (29%)
  matrix products  113 us (16%)
  local copies, waits for them, and re-layouts  81.8 us (11%)
  other arithmetic  63.1 us (9%)
  between operations  14.8 us (2%)
    all_gather x1, waiting for transfers between devices, body(): lax.all_gather(zx_delta.astype(jnp.bfloat16), 'dp', axis=0, tiled=True)  131 us
    psum x4, blocking collectives, body(): whole = lax.psum(partial_value, 'tp').astype(jnp.bfloat16)  109 us
    all_to_all x1, waiting for transfers between devices, body(): lax.all_to_all(zx_codes, 'tp', split_axis=2, concat_axis=0, tiled=True)  79.2 us
    psum x4, blocking collectives, body(): totals = lax.psum(squares[:, None] * group_mask, 'tp')  58.1 us
    all_gather x4, blocking collectives, body(): bc_all = lax.all_gather(conv_piece, 'tp', axis=1, tiled=True)  56.3 us
    dot_general x4, matrix products, body(): jnp.einsum('rhpn,rn->rhp', state, c_group, precision=lax.Precision.HIGHEST)  51.1 us
    dot_general x4, matrix products, body(): zx = jnp.dot(normed, zx_weights, preferred_element_type=jnp.float32)  40.7 us
    unnamed x30, local copies, waits for them, and re-layouts  27.7 us
  transfers between devices with their start and end apart: 3, of which 2 were waited for; matrix products, arithmetic and copies ran while one was open for 11% of the time, Pallas kernels for 0%

commit v1 on v0

--- a/solution.py
+++ b/solution.py
@@ -92,7 +92,14 @@
         dt_raw = jnp.dot(normed, w_dt, preferred_element_type=jnp.float32)
         conv_inner, history_x = conv_step(history_x, inner, conv_x)
         conv_piece, history_bc = conv_step(history_bc, bc_raw, conv_bc)
-        bc_all = lax.all_gather(conv_piece, "tp", axis=1, tiled=True)
+        ring = [conv_piece]
+        for hop in range(7):
+            ring.append(lax.ppermute(ring[-1], "tp", [(dev, (dev + 1) % 8) for dev in range(8)]))
+        bc_all = jnp.roll(
+            jnp.concatenate(ring[::-1], axis=1),
+            (lax.axis_index("tp") + 1) * ring[0].shape[1],
+            axis=1,
+        )
         b_group = lax.dynamic_slice_in_dim(bc_all, group * states_n, states_n, 1)
         c_group = lax.dynamic_slice_in_dim(bc_all, G * states_n + group * states_n, states_n, 1)
         step_size = jax.nn.softplus(dt_raw + dt_bias)

time: 721 us -> 770 us (1.068)
  waiting for transfers between devices: 210 us -> 315 us
  blocking collectives: 224 us -> 166 us
    ppermute x0 -> x28, waiting for transfers between devices: none -> 125 us  [body(): lax.ppermute(ring[-1], 'tp', [(dev, (dev + 1) % 8) for dev in range(8)])]
    all_gather x4 -> x0, blocking collectives: 56.3 us -> none  [body(): bc_all = lax.all_gather(conv_piece, 'tp', axis=1, tiled=True)]
    all_gather x1, waiting for transfers between devices: 131 us -> 111 us  [body(): lax.all_gather(zx_delta.astype(jnp.bfloat16), 'dp', axis=0, tiled=True)]
    unnamed x30 -> x58, local copies, waits for them, and re-layouts: 27.7 us -> 27.8 us
  transfers between devices with their start and end apart: 3 -> 31, of which waited for: 2 -> 28; matrix products, arithmetic and copies ran while one was open for 11% -> 13% of each run, Pallas kernels for 0% -> 0%
where the time goes in v1:
time: 770 us; the launch traced here: 761 us
  waiting for transfers between devices  315 us (41%)
  blocking collectives  166 us (22%)
  matrix products  113 us (15%)
  local copies, waits for them, and re-layouts  81.8 us (11%)
  other arithmetic  63.6 us (8%)
  between operations  15 us (2%)
    ppermute x28, waiting for transfers between devices, body(): lax.ppermute(ring[-1], 'tp', [(dev, (dev + 1) % 8) for dev in range(8)])  125 us
    all_gather x1, waiting for transfers between devices, body(): lax.all_gather(zx_delta.astype(jnp.bfloat16), 'dp', axis=0, tiled=True)  111 us
    psum x4, blocking collectives, body(): whole = lax.psum(partial_value, 'tp').astype(jnp.bfloat16)  109 us
    all_to_all x1, waiting for transfers between devices, body(): lax.all_to_all(zx_codes, 'tp', split_axis=2, concat_axis=0, tiled=True)  79.2 us
    psum x4, blocking collectives, body(): totals = lax.psum(squares[:, None] * group_mask, 'tp')  56.9 us
    dot_general x4, matrix products, body(): jnp.einsum('rhpn,rn->rhp', state, c_group, precision=lax.Precision.HIGHEST)  51.1 us
    dot_general x4, matrix products, body(): zx = jnp.dot(normed, zx_weights, preferred_element_type=jnp.float32)  40.7 us
    unnamed x58, local copies, waits for them, and re-layouts  27.8 us
  transfers between devices with their start and end apart: 31, of which 28 were waited for; matrix products, arithmetic and copies ran while one was open for 13% of the time, Pallas kernels for 0%

profile of v1, /device:TPU:0, one launch (start us, length us, event | category | flops | bytes accessed | tf_op | source)
XLA Modules:
  0.0 761.5 jit_solution(18243680015152721995)
XLA Ops:
  12.6 15.0 %copy.29 = bf16[128,2,8192]{0,1,2:T(2,128)(2,1)} copy(bf16[128,2,8192]{2,1,0:T(2,128)(2,1)} %param.24) | data formatting | bytes 8388608 | tf_op args[3]
  38.1 10.8 %mul.616 = f32[1024,2,1024]{2,1,0:T(2,128)} reshape(f32[8,128,2,8,128]{4,3,2,1,0:T(8,128)} %mul.615) | data formatting | bytes 16777216 | tf_op jit(solution)/shard_map/mul | solution.py:19
  48.8 79.2 %all-to-all-done = bf16[128,2,8192]{0,1,2:T(2,128)(2,1)} async-done(((bf16[128,2,8192]{0,1,2:T(2,128)(2,1)}), bf16[128,2,8192]{0,1,2:T(2,128)(2,1)}, u32[]{:S(2)}, u32[]{:S(2)}) %all-to-all-start) | async-done | bytes 4194336 | tf_op jit(solution)/shard_map/all_to_all | solution.py:58
  136.5 17.1 %copy.30 = f32[8,128,2,1024]{3,2,1,0:T(2,128)} copy(f32[8,128,2,1024]{1,2,3,0:T(2,128)} %convert_bitcast_fusion) | data formatting | bytes 16777216 | tf_op jit(solution)/shard_map/convert_element_type | solution.py:17
  198.0 10.1 %add_convert_fusion.1 = bf16[1024,4096]{1,0:T(8,128)(2,1)} fusion(bf16[1024,4096]{1,0:T(8,128)(2,1)} %all-gather.5.cloned.1.call-done, bf16[1024,4096]{1,0:T(8,128)(2,1)} %param.37), kind=kLoop, calls=%fused_computation.1 | loop fusion | flops 16777216 | bytes 25165824 | tf_op jit(solution)/shard_map/convert_element_type | solution.py:69
  208.1 111.1 %all-gather.3.cloned.1.call-done = bf16[4096,2,1024]{2,1,0:T(2,128)(2,1)} async-done(((bf16[1024,2,1024]{2,1,0:T(2,128)(2,1)}), bf16[4096,2,1024]{2,1,0:T(2,128)(2,1)}) %all-gather.3.cloned.1.call-update) | async-done | bytes 16777232 | tf_op jit(solution)/shard_map/all_gather | solution.py:61
  319.2 19.2 %add_convert_fusion = bf16[4096,2,1024]{2,1,0:T(2,128)(2,1)S(1)} fusion(bf16[4096,2,1024]{2,1,0:T(2,128)(2,1)} %all-gather.3.cloned.1.call-done, bf16[4096,2,1024]{2,1,0:T(2,128)(2,1)} %param.23), kind=kLoop, calls=%fused_computation | loop fusion | flops 33554432 | bytes 50331648 | tf_op jit(solution)/shard_map/convert_element_type | solution.py:64
  347.7 20.7 %copy.31 = bf16[2048,4096]{1,0:T(8,128)(2,1)} copy(bf16[2048,4096]{0,1:T(8,128)(2,1)} %bitcast.211) | data formatting | bytes 33554432 | tf_op jit(solution)/shard_map/dot_general | solution.py:87
  368.4 10.2 %fusion.29 = f32[8,2,1024]{2,0,1:T(8,128)S(1)} fusion(bf16[2,1024,4096]{2,1,0:T(8,128)(2,1)} %bitcast.206, f32[4096]{0:T(1024)S(1)} %copy-done.5, f32[8]{0:T(128)S(1)} %add_rsqrt_fusion.7, bf16[4,8,4096]{2,1,0:T(8,128)(2,1)S(1)} %copy-done.2), kind=kOutput, calls=%fused_computation.115 | convolution fusion | flops 134348800 | bytes 16925184 | tf_op jit(solution)/shard_map/dot_general | solution.py:87
  378.9 13.1 %fusion.1 = f32[8,1,16,64]{3,1,2,0:T(1,128)S(1)} fusion(f32[8,16,64,256]{3,2,1,0:T(8,128)} %param.35, f32[8,256]{1,0:T(8,128)S(1)} %get-tuple-element.24, f32[8,16,64]{2,1,0:T(8,128)S(1)} %broadcast_multiply_fusion.3, f32[8,16]{1,0:T(8,128)S(1)} %get-tuple-element.27, f32[8,256,1,1]{1,0,2,3:T(8,128)S(1)} %get-tuple-element.23), kind=kOutput, calls=%fused_computation.9 | convolution fusion | flops 31457280 | bytes 8471040 | tf_op jit(solution)/shard_map/rhpn,rn->rhp/dot_general | solution.py:113
  392.2 16.2 %psum.56 = f32[8,4]{0,1:T(4,128)S(1)} all-reduce(f32[8,4]{0,1:T(4,128)S(1)} %broadcast_multiply_fusion.7), channel_id=1, replica_groups=mesh['dp'=4,'tp'=8] {'tp'}, use_global_device_ids=true, to_apply=%region_4.6 | all-reduce | flops 32 | bytes 256 | tf_op jit(solution)/shard_map/psum | solution.py:118
  413.2 27.4 %all-reduce.4 = bf16[8,4096]{1,0:T(8,128)(2,1)S(1)} all-reduce(f32[8,4096]{1,0:T(8,128)S(1)} %fusion.84), channel_id=1, replica_groups=mesh['dp'=4,'tp'=8] {'tp'}, use_global_device_ids=true, to_apply=%region_6.8 | all-reduce | flops 32768 | bytes 196608 | tf_op jit(solution)/shard_map/psum | solution.py:122
  440.8 10.2 %fusion.35 = f32[8,2,1024]{2,0,1:T(8,128)S(1)} fusion(bf16[2,1024,4096]{2,1,0:T(8,128)(2,1)} %bitcast.207, bf16[8,4096]{1,0:T(8,128)(2,1)S(1)} %multiply_convert_fusion.2), kind=kOutput, calls=%fused_computation.120 | convolution fusion | flops 134217728 | bytes 16908288 | tf_op jit(solution)/shard_map/dot_general | solution.py:87
  486.0 13.7 %fusion.10 = f32[8,1,16,64]{3,1,2,0:T(1,128)S(1)} fusion(f32[8,16,64,256]{3,2,1,0:T(8,128)} %param.35, f32[8,256]{1,0:T(8,128)S(1)} %get-tuple-element.20, f32[8,16,64]{2,1,0:T(8,128)S(1)} %broadcast_multiply_fusion.2, f32[8,16]{1,0:T(8,128)S(1)} %get-tuple-element.29, f32[8,256]{1,0:T(8,128)S(1)} %get-tuple-element.24, ...), kind=kOutput, calls=%fused_computation.19 | convolution fusion | flops 37748736 | bytes 8512512 | tf_op jit(solution)/shard_map/rhpn,rn->rhp/dot_general | solution.py:113
  500.0 13.6 %psum.58 = f32[8,4]{0,1:T(4,128)S(1)} all-reduce(f32[8,4]{0,1:T(4,128)S(1)} %broadcast_multiply_fusion.6), channel_id=1, replica_groups=mesh['dp'=4,'tp'=8] {'tp'}, use_global_device_ids=true, to_apply=%region_11.13 | all-reduce | flops 32 | bytes 256 | tf_op jit(solution)/shard_map/psum | solution.py:118
  518.3 27.1 %all-reduce.5 = bf16[8,4096]{1,0:T(8,128)(2,1)S(1)} all-reduce(f32[8,4096]{1,0:T(8,128)S(1)} %fusion.82), channel_id=1, replica_groups=mesh['dp'=4,'tp'=8] {'tp'}, use_global_device_ids=true, to_apply=%region_13.15 | all-reduce | flops 32768 | bytes 196608 | tf_op jit(solution)/shard_map/psum | solution.py:122
  546.6 10.2 %fusion.33 = f32[8,2,1024]{2,0,1:T(8,128)S(1)} fusion(bf16[2,1024,4096]{2,1,0:T(8,128)(2,1)} %bitcast.208, bf16[8,4096]{1,0:T(8,128)(2,1)S(1)} %multiply_convert_fusion.1), kind=kOutput, calls=%fused_computation.118 | convolution fusion | flops 134217728 | bytes 16908288 | tf_op jit(solution)/shard_map/dot_general | solution.py:87
  586.2 14.5 %fusion.2 = f32[8,1,16,64]{3,1,2,0:T(1,128)S(1)} fusion(f32[8,256]{1,0:T(8,128)S(1)} %get-tuple-element.16, f32[8,16,64]{2,1,0:T(8,128)S(1)} %broadcast_multiply_fusion.1, f32[8,16]{1,0:T(8,128)S(1)} %get-tuple-element.31, f32[8,16,64,256]{3,2,1,0:T(8,128)} %param.35, f32[8,256]{1,0:T(8,128)S(1)} %get-tuple-element.20, ...), kind=kOutput, calls=%fused_computation.10 | convolution fusion | flops 44040192 | bytes 8553984 | tf_op jit(solution)/shard_map/rhpn,rn->rhp/dot_general | solution.py:113
  601.0 13.6 %psum.60 = f32[8,4]{0,1:T(4,128)S(1)} all-reduce(f32[8,4]{0,1:T(4,128)S(1)} %broadcast_multiply_fusion.5), channel_id=1, replica_groups=mesh['dp'=4,'tp'=8] {'tp'}, use_global_device_ids=true, to_apply=%region_18.20 | all-reduce | flops 32 | bytes 256 | tf_op jit(solution)/shard_map/psum | solution.py:118
  619.4 27.1 %all-reduce.6 = bf16[8,4096]{1,0:T(8,128)(2,1)S(1)} all-reduce(f32[8,4096]{1,0:T(8,128)S(1)} %fusion.80), channel_id=1, replica_groups=mesh['dp'=4,'tp'=8] {'tp'}, use_global_device_ids=true, to_apply=%region_20.22 | all-reduce | flops 32768 | bytes 196608 | tf_op jit(solution)/shard_map/psum | solution.py:122
  652.2 10.2 %fusion.31 = f32[8,2,1024]{2,0,1:T(8,128)S(1)} fusion(bf16[2,1024,4096]{2,1,0:T(8,128)(2,1)} %bitcast.209, bf16[8,4096]{1,0:T(8,128)(2,1)S(1)} %multiply_convert_fusion), kind=kOutput, calls=%fused_computation.116 | convolution fusion | flops 134217728 | bytes 16908288 | tf_op jit(solution)/shard_map/dot_general | solution.py:87
  698.2 9.8 %fusion.107 = f32[8,1,16,64]{3,1,2,0:T(1,128)S(1)} fusion(f32[8,16,64,256]{3,2,1,0:T(8,128)S(1)} %multiply_add_fusion, f32[8,256,1,1]{1,0,2,3:T(8,128)S(1)} %get-tuple-element.11), kind=kOutput, calls=%fused_computation.228 | convolution fusion | flops 25165824 | bytes 8429568 | tf_op jit(solution)/shard_map/rhpn,rn->rhp/dot_general | solution.py:113
  708.3 13.6 %psum.62 = f32[8,4]{0,1:T(4,128)S(1)} all-reduce(f32[8,4]{0,1:T(4,128)S(1)} %broadcast_multiply_fusion.4), channel_id=1, replica_groups=mesh['dp'=4,'tp'=8] {'tp'}, use_global_device_ids=true, to_apply=%region_25.27 | all-reduce | flops 32 | bytes 256 | tf_op jit(solution)/shard_map/psum | solution.py:118
  726.7 27.1 %all-reduce.7 = bf16[8,4096]{1,0:T(8,128)(2,1)S(1)} all-reduce(f32[8,4096]{1,0:T(8,128)S(1)} %fusion.78), channel_id=1, replica_groups=mesh['dp'=4,'tp'=8] {'tp'}, use_global_device_ids=true, to_apply=%region_27.29 | all-reduce | flops 32768 | bytes 196608 | tf_op jit(solution)/shard_map/psum | solution.py:122
  (225 shorter events, 205.8 us)
Async XLA Ops:
  7.2 190.8 %all-gather.5.cloned.1.call-start = ((), (), s32[]{:S(2)}) async-start(), calls=%async_computation.2 | async-start | bytes 10485760 | tf_op jit(solution)/shard_map/all_gather | solution.py:68
  27.6 100.5 %all-to-all-start = ((bf16[128,2,8192]{0,1,2:T(2,128)(2,1)}), bf16[128,2,8192]{0,1,2:T(2,128)(2,1)}, u32[]{:S(2)}, u32[]{:S(2)}) async-start(bf16[128,2,8192]{0,1,2:T(2,128)(2,1)} %copy.29), calls=%async_computation | async-start | bytes 8388608 | tf_op jit(solution)/shard_map/all_to_all | solution.py:58
  34.0 285.2 %all-gather.3.cloned.1.call-start = ((), (), s32[]{:S(2)}) async-start(), calls=%async_computation.1 | async-start | bytes 20971520 | tf_op jit(solution)/shard_map/all_gather | solution.py:61
  163.5 4.9 collective-permute-start
  168.4 4.9 collective-permute-start.1
  173.3 4.9 collective-permute-start.2
  178.2 4.9 collective-permute-start.3
  183.0 4.9 collective-permute-start.4
  187.9 4.9 collective-permute-start.5
  192.8 5.0 collective-permute-start.6
  451.6 4.9 collective-permute-start.7
  456.6 4.9 collective-permute-start.8
  476.1 4.9 collective-permute-start.12
  480.9 4.9 collective-permute-start.13
  546.2 10.7 %collective-permute-start.14 = (f32[8,256]{1,0:T(8,128)S(1)}, f32[8,256]{1,0:T(8,128)S(1)}, u32[]{:S(2)}, u32[]{:S(2)}) collective-permute-start(f32[8,256]{1,0:T(8,128)S(1)} %divide_multiply_fusion.5), channel_id=1, source_target_pairs={{0,1},{1,2},{2,3},{3,4},{4,5},{5,6},{6,7},{7,0},{8,9},{9,10},{10,1... | collective-permute-start | bytes 24584 | tf_op jit(solution)/shard_map/ppermute | solution.py:97
  556.8 4.9 collective-permute-start.15
  561.7 4.9 collective-permute-start.16
  566.6 4.9 collective-permute-start.17
  571.5 4.9 collective-permute-start.18
  576.3 4.9 collective-permute-start.19
  647.2 4.9 collective-permute-start.21
  652.2 10.2 %collective-permute-start.22 = (f32[8,256]{1,0:T(8,128)S(1)}, f32[8,256]{1,0:T(8,128)S(1)}, u32[]{:S(2)}, u32[]{:S(2)}) collective-permute-start(f32[8,256]{1,0:T(8,128)S(1)} %collective-permute-done.21), channel_id=1, source_target_pairs={{0,1},{1,2},{2,3},{3,4},{4,5},{5,6},{6,7},{7,0},{8,9},{9,10},{10,1... | collective-permute-start | bytes 24584 | tf_op jit(solution)/shard_map/ppermute | solution.py:97
  662.4 4.9 collective-permute-start.23
  681.9 5.0 collective-permute-start.27
  (21 other events, 437.5 us)
Sparse Core Ops, SparseCore 0:
  12.7 90.1 all-gather.4
  162.9 156.2 all-gather.2
